TPU v7x, 32 devices: a whole 2x2x4 slice. The times are simulated.
32 devices in a mesh: event: 4 (over z), terrain: 8 (over y, x, core).
Axes of the slice: x: 2, y: 2, z: 4, core: 2. Of those that a mesh axis runs over, the one named last changes fastest.
Arguments:
- level_start: float32 [4, 256, 1024], P('event', 'terrain'), may hold values from -18 to 18
- bed_depth: float32 [256, 1024], P('terrain'), may hold values from 0.5 to 2
- wet_bits: int32 [4, 256, 1024], P('event', 'terrain'), may hold values from 0 to 255
- tile_owner: int32 [2048, 1], P('terrain'), may hold values from 0 to 7; in each aligned block of 256 rows (0 to 255, 256 to 511, ...) at most 48 rows name the same one
- vuln_weight: bfloat16 [128, 256], replicated, may hold values from -0.5 to 0.5
- vuln_bias: float32 [256], replicated, may hold values from -2 to 2
- account_index: int32 [3072, 128], P('terrain'), may hold values from 0 to 1023
- bin_index: int32 [3072, 128], P('terrain'), may hold values from 0 to 255
- exposure_value: bfloat16 [3072, 128], P('terrain'), may hold values from 1 to 10
- deductible: float32 [1024], replicated, may hold values from 0 to 0.8
- limit: float32 [1024], replicated, may hold values from 0.5 to 1.5
Outputs:
- level: float32 [4, 256, 1024], P('event', 'terrain')
- net_loss: bfloat16 [4, 1024, 256], P('event')
- portfolio: float32 [1024, 256], P('terrain')
Inputs may be any that keep to these rules, and one draw needn't show every extreme that they name: `tile_owner`: among the 256 tiles of one device no owner is named more than 48 times; in some devices one owner is named exactly 48 times. `wet_bits`: bit s (the value // 2**s, mod 2) is 1 where the cell is wet in substep s. `account_index`: rows of an owner's records that no tile reaches are not read.
All inputs are finite; a program needn't handle non-finite values.
Results may differ from a plain program's by a relative error of at most 0.0004.
The roundings to bfloat16 on the way count: a program that leaves them out, or rounds other values in their place, can miss the bound.
Values may be sent and summed in bfloat16 or wider, within the bound.
A program may use at most 64 MiB of HBM per device.

v0:
```python
import jax
import jax.numpy as jnp
from jax import lax
from jax.sharding import PartitionSpec as P

SUBSTEPS = 8
courant = 0.5
gravity = 1.0


def with_halo(cells, sides, width):
    for axis, dim in sides:
        count = lax.axis_size(axis)
        ends = count - 1
        head = lax.slice_in_dim(cells, 0, width, axis=dim)
        tail = lax.slice_in_dim(cells, cells.shape[dim] - width, cells.shape[dim], axis=dim)
        cells = jnp.concatenate(
            [
                lax.ppermute(tail, axis, [(i, (i + 1) % count) for i in range(ends)]),
                cells,
                lax.ppermute(head, axis, [((i + 1) % count, i) for i in range(ends)]),
            ],
            axis=dim,
        )
    return cells


def pad_columns(field):
    return jnp.pad(field[:, 1:-1, :], ((0, 0), (0, 0), (1, 1)))


def neighbour_mean(field):
    inner = pad_columns(field)
    return 0.25 * (field[:, 2:, :] + field[:, :-2, :] + inner[:, :, 2:] + inner[:, :, :-2])


def friedrichs_step(level, row_speed, col_speed, bed_depth, wet_factor):
    row_flow = bed_depth * row_speed
    col_flow = pad_columns(bed_depth * col_speed)
    level_pad = pad_columns(level)
    new_level = neighbour_mean(level) - 0.5 * courant * (
        row_flow[:, 2:, :] - row_flow[:, :-2, :] + (col_flow[:, :, 2:] - col_flow[:, :, :-2])
    )
    new_row = (
        neighbour_mean(row_speed) - 0.5 * courant * gravity * (level[:, 2:, :] - level[:, :-2, :])
    ) * wet_factor
    new_col = (
        neighbour_mean(col_speed)
        - 0.5 * courant * gravity * (level_pad[:, :, 2:] - level_pad[:, :, :-2])
    ) * wet_factor
    return (new_level, new_row, new_col)


def per_device(
    level_start,
    bed_depth,
    wet_bits,
    tile_owner,
    vuln_weight,
    vuln_bias,
    account_index,
    bin_index,
    exposure_value,
    deductible,
    limit,
):
    groups, rows, width = level_start.shape
    tile_cells, bin_count = vuln_weight.shape
    account_count = deductible.shape[0]
    owners = lax.axis_size("terrain")
    zeros = jnp.zeros_like(level_start)
    fields = jnp.stack([level_start, zeros, zeros, jnp.broadcast_to(bed_depth, level_start.shape)])
    widened = with_halo(fields, (("terrain", 2),), SUBSTEPS)
    wet_wide = with_halo(wet_bits, (("terrain", 1),), SUBSTEPS)
    level, row_speed, col_speed = (widened[0], widened[1], widened[2])
    bed_wide = widened[3][0]
    first_row = lax.axis_index("terrain") * rows - SUBSTEPS
    total_rows = rows * owners
    for step in range(SUBSTEPS):
        remain = SUBSTEPS - step - 1
        out_rows = rows + 2 * remain
        bed_now = bed_wide[step : step + out_rows + 2]
        row_ids = first_row + step + 1 + jnp.arange(out_rows, dtype=jnp.int32)
        inside = ((row_ids >= 0) & (row_ids < total_rows)).astype(jnp.float32)[None, :, None]
        wet_factor = (wet_wide[:, step + 1 : step + 1 + out_rows] // 2**step % 2).astype(
            jnp.float32
        ) * inside
        level, row_speed, col_speed = friedrichs_step(
            level, row_speed, col_speed, bed_now, wet_factor
        )
        level = level * inside
    pieces = level.astype(jnp.bfloat16).reshape(-1, tile_cells)
    slot_count = account_index.shape[0]
    capacity = slot_count // owners
    owner = tile_owner[:, 0]
    onehot = (owner[:, None] == jnp.arange(owners, dtype=jnp.int32)[None, :]).astype(jnp.int32)
    rank = jnp.sum((jnp.cumsum(onehot, axis=0) - onehot) * onehot, axis=1)
    place = owner * capacity + rank
    chosen = (place[:, None] == jnp.arange(slot_count, dtype=jnp.int32)[None, :]).astype(
        jnp.float32
    )
    marks_out = jnp.sum(chosen, axis=0).astype(jnp.bfloat16).reshape(owners, capacity)
    chosen = chosen.astype(jnp.bfloat16)
    pick = (((0,), (0,)), ((), ()))
    local_ratio = jax.nn.sigmoid(
        jnp.dot(pieces, vuln_weight, preferred_element_type=jnp.float32) + vuln_bias
    ).astype(jnp.bfloat16)
    outgoing = (
        lax.dot_general(chosen, local_ratio, pick, preferred_element_type=jnp.float32)
        .astype(jnp.bfloat16)
        .reshape(owners, capacity, bin_count)
    )
    ratio, marks = (
        lax.all_to_all(outgoing, "terrain", split_axis=0, concat_axis=0, tiled=True),
        lax.all_to_all(marks_out, "terrain", split_axis=0, concat_axis=0, tiled=True),
    )
    weighted = ratio.reshape(slot_count, bin_count) * marks.reshape(slot_count)[:, None]
    block = 32
    bin_range = jnp.arange(bin_count, dtype=jnp.int32)
    share_rows = account_count // owners
    lower = lax.axis_index("terrain") * share_rows
    scale = account_count / (rows * width * owners)
    columns = jnp.arange(account_count, dtype=jnp.int32)

    def add_block(total, block_id):
        first = block_id * block
        account_part = lax.dynamic_slice_in_dim(account_index, first, block, 0).reshape(-1)
        value_part = lax.dynamic_slice_in_dim(exposure_value, first, block, 0).reshape(-1)
        threshold_part = lax.dynamic_slice_in_dim(bin_index, first, block, 0)
        ratio_part = lax.dynamic_slice_in_dim(weighted, first, block, 0)
        left = jnp.where(
            account_part[:, None] == columns[None, :],
            value_part[:, None],
            jnp.zeros((), jnp.bfloat16),
        )
        right = jnp.where(
            bin_range[None, None, :] >= threshold_part[:, :, None],
            ratio_part[:, None, :],
            jnp.zeros((), jnp.bfloat16),
        ).reshape(-1, bin_count)
        return (
            total + lax.dot_general(left, right, pick, preferred_element_type=jnp.float32),
            None,
        )

    total, _ = lax.scan(
        add_block,
        jnp.zeros((account_count, bin_count), jnp.float32),
        jnp.arange(slot_count // block, dtype=jnp.int32),
    )
    whole = lax.psum(total, "terrain")
    net_whole = jnp.minimum(jnp.maximum(whole * scale - deductible[:, None], 0.0), limit[:, None])
    net_loss = net_whole.astype(jnp.bfloat16)[None]
    net_share = lax.dynamic_slice_in_dim(net_whole, lower, share_rows, 0)
    portfolio = lax.psum(net_share, "event") / (groups * lax.axis_size("event"))
    return (level, net_loss, portfolio)


def solution(mesh):
    placed = (
        P("event", "terrain", None),
        P("terrain", None),
        P("event", "terrain", None),
        P("terrain", None),
        P(),
        P(),
        P("terrain", None),
        P("terrain", None),
        P("terrain", None),
        P(),
        P(),
    )
    return jax.shard_map(
        per_device,
        mesh=mesh,
        in_specs=placed,
        out_specs=(P("event", "terrain", None), P("event", None, None), P("terrain", None)),
        check_vma=False,
    )
```

profile of v0, /device:TPU:0, one launch (start us, length us, event | category | flops | bytes accessed | tf_op | source)
XLA Modules:
  0.0 240.6 jit_solution(13161614519495146786)
XLA Ops:
  7.2 0.8 pad_maximum_fusion.3
  8.0 1.3 collective-permute-start.1
  9.3 3.0 %collective-permute-start = (f32[4,1,8,1024]{3,2,1,0:T(8,128)S(1)}, f32[4,1,8,1024]{3,2,1,0:T(8,128)S(1)}, u32[]{:S(2)}, u32[]{:S(2)}) collective-permute-start(f32[4,1,8,1024]{3,2,1,0:T(8,128)S(1)} %get-tuple-element.117), channel_id=1, source_target_pairs={{0,1},{1,2},{2,3},{3,4},{4,5},{5,6},{6,7},{8,9},{9,10},{10,11},{11... | collective-permute-start | bytes 393224 | tf_op jit(solution)/shard_map/ppermute | solution.py:19
  12.4 0.8 fusion.195
  13.2 4.5 %collective-permute-start.2 = (s32[1,8,1024]{2,1,0:T(8,128)S(1)}, s32[1,8,1024]{2,1,0:T(8,128)S(1)}, u32[]{:S(2)}, u32[]{:S(2)}) collective-permute-start(s32[1,8,1024]{2,1,0:T(8,128)S(1)} %get-tuple-element.152), channel_id=1, source_target_pairs={{0,1},{1,2},{2,3},{3,4},{4,5},{5,6},{6,7},{8,9},{9,10},{10,11},{11... | collective-permute-start | bytes 98312 | tf_op jit(solution)/shard_map/ppermute | solution.py:19
  17.7 1.3 collective-permute-start.3
  20.5 0.8 fusion.174
  22.7 5.3 %all-to-all-start.1 = ((bf16[8,1,48]{2,1,0:T(2,128)(2,1)}), bf16[8,1,48]{2,1,0:T(2,128)(2,1)S(1)}, u32[]{:S(2)}, u32[]{:S(2)}) async-start(bf16[8,1,48]{2,1,0:T(2,128)(2,1)} %convert_element_type.186), calls=%async_computation.1 | async-start | bytes 8192 | tf_op jit(solution)/shard_map/all_to_all | solution.py:115
  28.2 0.9 constant_dynamic-update-slice_fusion.1
  29.2 1.0 pad_maximum_fusion
  35.3 0.9 fusion.184
  36.2 1.1 convolution_convert_fusion
  37.3 4.2 %all-to-all-start = ((bf16[8,48,256]{2,1,0:T(8,128)(2,1)}), bf16[8,48,256]{2,1,0:T(8,128)(2,1)S(1)}, u32[]{:S(2)}, u32[]{:S(2)}) async-start(bf16[8,48,256]{2,1,0:T(8,128)(2,1)} %bitcast.19), calls=%async_computation | async-start | bytes 393216 | tf_op jit(solution)/shard_map/all_to_all | solution.py:114
  41.7 6.0 %all-to-all-done = bf16[8,48,256]{2,1,0:T(8,128)(2,1)S(1)} async-done(((bf16[8,48,256]{2,1,0:T(8,128)(2,1)}), bf16[8,48,256]{2,1,0:T(8,128)(2,1)S(1)}, u32[]{:S(2)}, u32[]{:S(2)}) %all-to-all-start) | async-done | bytes 196640 | tf_op jit(solution)/shard_map/all_to_all | solution.py:114
  47.9 90.0 %while.11 = (s32[]{:T(128)}, f32[1024,256]{1,0:T(8,128)S(1)}, s32[12]{0:T(128)S(1)}, s32[384,128]{1,0:T(8,128)}, bf16[384,128]{1,0:T(8,128)(2,1)}, /*index=5*/s3...) while((s32[]{:T(128)}, f32[1024,256]{1,0:T(8,128)S(1)}, ...), condition=%wide.region_5.6_spmd.clone, body=%wide.region_4.5_spmd.clone.sunk | while | flops 2158493696 | bytes 6463685 | solution.py:146
  50.8 4.6 %fusion.203 = f32[1024,256]{1,0:T(8,128)S(1)} fusion(bf16[4096,256]{1,0:T(8,128)(2,1)S(1)} %bitcast.77, s32[4096]{0:T(1024)S(1)} %get-tuple-element.201, s32[4096]{0:T(1024)S(1)} %get-tuple-element.202, bf16[4096]{0:T(1024)(128)(2,1)S(1)} %dynamic-slice_bitcast_fusion.6, f32[1024,256]{1,0:T(8,128)S(1)} %get-tuple-element.215, pred[]{:T(512)S(6)} %compare.53), kind=kOutput, calls=%fused_computation.11.clone.1 | convolution fusion | flops 2158493696 | bytes 4235265 | tf_op jit(solution)/shard_map/while/body/eval_jaxpr/dot_general | solution.py:142
  58.3 4.6 %fusion.203 = f32[1024,256]{1,0:T(8,128)S(1)} fusion(bf16[4096,256]{1,0:T(8,128)(2,1)S(1)} %bitcast.77, s32[4096]{0:T(1024)S(1)} %get-tuple-element.201, s32[4096]{0:T(1024)S(1)} %get-tuple-element.202, bf16[4096]{0:T(1024)(128)(2,1)S(1)} %dynamic-slice_bitcast_fusion.6, f32[1024,256]{1,0:T(8,128)S(1)} %get-tuple-element.215, pred[]{:T(512)S(6)} %compare.53), kind=kOutput, calls=%fused_computation.11.clone.1 | convolution fusion | flops 2158493696 | bytes 4235265 | tf_op jit(solution)/shard_map/while/body/eval_jaxpr/dot_general | solution.py:142
  65.8 4.6 %fusion.203 = f32[1024,256]{1,0:T(8,128)S(1)} fusion(bf16[4096,256]{1,0:T(8,128)(2,1)S(1)} %bitcast.77, s32[4096]{0:T(1024)S(1)} %get-tuple-element.201, s32[4096]{0:T(1024)S(1)} %get-tuple-element.202, bf16[4096]{0:T(1024)(128)(2,1)S(1)} %dynamic-slice_bitcast_fusion.6, f32[1024,256]{1,0:T(8,128)S(1)} %get-tuple-element.215, pred[]{:T(512)S(6)} %compare.53), kind=kOutput, calls=%fused_computation.11.clone.1 | convolution fusion | flops 2158493696 | bytes 4235265 | tf_op jit(solution)/shard_map/while/body/eval_jaxpr/dot_general | solution.py:142
  73.3 4.6 %fusion.203 = f32[1024,256]{1,0:T(8,128)S(1)} fusion(bf16[4096,256]{1,0:T(8,128)(2,1)S(1)} %bitcast.77, s32[4096]{0:T(1024)S(1)} %get-tuple-element.201, s32[4096]{0:T(1024)S(1)} %get-tuple-element.202, bf16[4096]{0:T(1024)(128)(2,1)S(1)} %dynamic-slice_bitcast_fusion.6, f32[1024,256]{1,0:T(8,128)S(1)} %get-tuple-element.215, pred[]{:T(512)S(6)} %compare.53), kind=kOutput, calls=%fused_computation.11.clone.1 | convolution fusion | flops 2158493696 | bytes 4235265 | tf_op jit(solution)/shard_map/while/body/eval_jaxpr/dot_general | solution.py:142
  80.8 4.6 %fusion.203 = f32[1024,256]{1,0:T(8,128)S(1)} fusion(bf16[4096,256]{1,0:T(8,128)(2,1)S(1)} %bitcast.77, s32[4096]{0:T(1024)S(1)} %get-tuple-element.201, s32[4096]{0:T(1024)S(1)} %get-tuple-element.202, bf16[4096]{0:T(1024)(128)(2,1)S(1)} %dynamic-slice_bitcast_fusion.6, f32[1024,256]{1,0:T(8,128)S(1)} %get-tuple-element.215, pred[]{:T(512)S(6)} %compare.53), kind=kOutput, calls=%fused_computation.11.clone.1 | convolution fusion | flops 2158493696 | bytes 4235265 | tf_op jit(solution)/shard_map/while/body/eval_jaxpr/dot_general | solution.py:142
  88.3 4.6 %fusion.203 = f32[1024,256]{1,0:T(8,128)S(1)} fusion(bf16[4096,256]{1,0:T(8,128)(2,1)S(1)} %bitcast.77, s32[4096]{0:T(1024)S(1)} %get-tuple-element.201, s32[4096]{0:T(1024)S(1)} %get-tuple-element.202, bf16[4096]{0:T(1024)(128)(2,1)S(1)} %dynamic-slice_bitcast_fusion.6, f32[1024,256]{1,0:T(8,128)S(1)} %get-tuple-element.215, pred[]{:T(512)S(6)} %compare.53), kind=kOutput, calls=%fused_computation.11.clone.1 | convolution fusion | flops 2158493696 | bytes 4235265 | tf_op jit(solution)/shard_map/while/body/eval_jaxpr/dot_general | solution.py:142
  95.8 4.6 %fusion.203 = f32[1024,256]{1,0:T(8,128)S(1)} fusion(bf16[4096,256]{1,0:T(8,128)(2,1)S(1)} %bitcast.77, s32[4096]{0:T(1024)S(1)} %get-tuple-element.201, s32[4096]{0:T(1024)S(1)} %get-tuple-element.202, bf16[4096]{0:T(1024)(128)(2,1)S(1)} %dynamic-slice_bitcast_fusion.6, f32[1024,256]{1,0:T(8,128)S(1)} %get-tuple-element.215, pred[]{:T(512)S(6)} %compare.53), kind=kOutput, calls=%fused_computation.11.clone.1 | convolution fusion | flops 2158493696 | bytes 4235265 | tf_op jit(solution)/shard_map/while/body/eval_jaxpr/dot_general | solution.py:142
  103.3 4.6 %fusion.203 = f32[1024,256]{1,0:T(8,128)S(1)} fusion(bf16[4096,256]{1,0:T(8,128)(2,1)S(1)} %bitcast.77, s32[4096]{0:T(1024)S(1)} %get-tuple-element.201, s32[4096]{0:T(1024)S(1)} %get-tuple-element.202, bf16[4096]{0:T(1024)(128)(2,1)S(1)} %dynamic-slice_bitcast_fusion.6, f32[1024,256]{1,0:T(8,128)S(1)} %get-tuple-element.215, pred[]{:T(512)S(6)} %compare.53), kind=kOutput, calls=%fused_computation.11.clone.1 | convolution fusion | flops 2158493696 | bytes 4235265 | tf_op jit(solution)/shard_map/while/body/eval_jaxpr/dot_general | solution.py:142
  110.8 4.6 %fusion.203 = f32[1024,256]{1,0:T(8,128)S(1)} fusion(bf16[4096,256]{1,0:T(8,128)(2,1)S(1)} %bitcast.77, s32[4096]{0:T(1024)S(1)} %get-tuple-element.201, s32[4096]{0:T(1024)S(1)} %get-tuple-element.202, bf16[4096]{0:T(1024)(128)(2,1)S(1)} %dynamic-slice_bitcast_fusion.6, f32[1024,256]{1,0:T(8,128)S(1)} %get-tuple-element.215, pred[]{:T(512)S(6)} %compare.53), kind=kOutput, calls=%fused_computation.11.clone.1 | convolution fusion | flops 2158493696 | bytes 4235265 | tf_op jit(solution)/shard_map/while/body/eval_jaxpr/dot_general | solution.py:142
  118.3 4.6 %fusion.203 = f32[1024,256]{1,0:T(8,128)S(1)} fusion(bf16[4096,256]{1,0:T(8,128)(2,1)S(1)} %bitcast.77, s32[4096]{0:T(1024)S(1)} %get-tuple-element.201, s32[4096]{0:T(1024)S(1)} %get-tuple-element.202, bf16[4096]{0:T(1024)(128)(2,1)S(1)} %dynamic-slice_bitcast_fusion.6, f32[1024,256]{1,0:T(8,128)S(1)} %get-tuple-element.215, pred[]{:T(512)S(6)} %compare.53), kind=kOutput, calls=%fused_computation.11.clone.1 | convolution fusion | flops 2158493696 | bytes 4235265 | tf_op jit(solution)/shard_map/while/body/eval_jaxpr/dot_general | solution.py:142
  125.8 4.6 %fusion.203 = f32[1024,256]{1,0:T(8,128)S(1)} fusion(bf16[4096,256]{1,0:T(8,128)(2,1)S(1)} %bitcast.77, s32[4096]{0:T(1024)S(1)} %get-tuple-element.201, s32[4096]{0:T(1024)S(1)} %get-tuple-element.202, bf16[4096]{0:T(1024)(128)(2,1)S(1)} %dynamic-slice_bitcast_fusion.6, f32[1024,256]{1,0:T(8,128)S(1)} %get-tuple-element.215, pred[]{:T(512)S(6)} %compare.53), kind=kOutput, calls=%fused_computation.11.clone.1 | convolution fusion | flops 2158493696 | bytes 4235265 | tf_op jit(solution)/shard_map/while/body/eval_jaxpr/dot_general | solution.py:142
  133.3 4.6 %fusion.203 = f32[1024,256]{1,0:T(8,128)S(1)} fusion(bf16[4096,256]{1,0:T(8,128)(2,1)S(1)} %bitcast.77, s32[4096]{0:T(1024)S(1)} %get-tuple-element.201, s32[4096]{0:T(1024)S(1)} %get-tuple-element.202, bf16[4096]{0:T(1024)(128)(2,1)S(1)} %dynamic-slice_bitcast_fusion.6, f32[1024,256]{1,0:T(8,128)S(1)} %get-tuple-element.215, pred[]{:T(512)S(6)} %compare.53), kind=kOutput, calls=%fused_computation.11.clone.1 | convolution fusion | flops 2158493696 | bytes 4235265 | tf_op jit(solution)/shard_map/while/body/eval_jaxpr/dot_general | solution.py:142
  137.9 1.0 copy-done.1
  139.0 56.2 %all-reduce.33.cloned.1.call-done = f32[1024,256]{1,0:T(8,128)} async-done(((f32[1024,256]{1,0:T(8,128)}), f32[1024,256]{1,0:T(8,128)}) %all-reduce.33.cloned.1.call-update) | async-done | bytes 1048592 | tf_op jit(solution)/shard_map/psum | solution.py:151
  195.2 2.4 convert_bitcast_fusion
  198.2 34.0 %all-reduce.35.cloned.1.call-done = f32[128,256]{1,0:T(8,128)} async-done(((f32[128,256]{1,0:T(8,128)}), f32[128,256]{1,0:T(8,128)}) %all-reduce.35.cloned.1.call-update) | async-done | bytes 131088 | tf_op jit(solution)/shard_map/psum | solution.py:155
  232.2 1.6 broadcast_multiply_fusion
  (144 shorter events, 35.1 us)
Async XLA Ops:
  7.2 29.1 %copy-start = (bf16[128,256]{1,0:T(8,128)(2,1)S(1)}, bf16[128,256]{1,0:T(8,128)(2,1)}, u32[]{:S(2)}) copy-start(bf16[128,256]{1,0:T(8,128)(2,1)} %param.17) | copy-start | bytes 196612
  8.0 21.1 %collective-permute-start.1 = (f32[4,1,8,1024]{3,2,1,0:T(8,128)S(1)}, f32[4,1,8,1024]{3,2,1,0:T(8,128)S(1)}, u32[]{:S(2)}, u32[]{:S(2)}) collective-permute-start(f32[4,1,8,1024]{3,2,1,0:T(8,128)S(1)} %get-tuple-element.118), channel_id=1, source_target_pairs={{1,0},{2,1},{3,2},{4,3},{5,4},{6,5},{7,6},{9,8},{10,9},{11,10},{12... | collective-permute-start | bytes 393224 | tf_op jit(solution)/shard_map/ppermute | solution.py:21
  9.3 19.8 %collective-permute-start = (f32[4,1,8,1024]{3,2,1,0:T(8,128)S(1)}, f32[4,1,8,1024]{3,2,1,0:T(8,128)S(1)}, u32[]{:S(2)}, u32[]{:S(2)}) collective-permute-start(f32[4,1,8,1024]{3,2,1,0:T(8,128)S(1)} %get-tuple-element.117), channel_id=1, source_target_pairs={{0,1},{1,2},{2,3},{3,4},{4,5},{5,6},{6,7},{8,9},{9,10},{10,11},{11... | collective-permute-start | bytes 393224 | tf_op jit(solution)/shard_map/ppermute | solution.py:19
  13.2 15.0 %collective-permute-start.2 = (s32[1,8,1024]{2,1,0:T(8,128)S(1)}, s32[1,8,1024]{2,1,0:T(8,128)S(1)}, u32[]{:S(2)}, u32[]{:S(2)}) collective-permute-start(s32[1,8,1024]{2,1,0:T(8,128)S(1)} %get-tuple-element.152), channel_id=1, source_target_pairs={{0,1},{1,2},{2,3},{3,4},{4,5},{5,6},{6,7},{8,9},{9,10},{10,11},{11... | collective-permute-start | bytes 98312 | tf_op jit(solution)/shard_map/ppermute | solution.py:19
  17.7 11.5 %collective-permute-start.3 = (s32[1,8,1024]{2,1,0:T(8,128)S(1)}, s32[1,8,1024]{2,1,0:T(8,128)S(1)}, u32[]{:S(2)}, u32[]{:S(2)}) collective-permute-start(s32[1,8,1024]{2,1,0:T(8,128)S(1)} %get-tuple-element.151), channel_id=1, source_target_pairs={{1,0},{2,1},{3,2},{4,3},{5,4},{6,5},{7,6},{9,8},{10,9},{11,10},{12... | collective-permute-start | bytes 98312 | tf_op jit(solution)/shard_map/ppermute | solution.py:21
  22.7 14.6 %all-to-all-start.1 = ((bf16[8,1,48]{2,1,0:T(2,128)(2,1)}), bf16[8,1,48]{2,1,0:T(2,128)(2,1)S(1)}, u32[]{:S(2)}, u32[]{:S(2)}) async-start(bf16[8,1,48]{2,1,0:T(2,128)(2,1)} %convert_element_type.186), calls=%async_computation.1 | async-start | bytes 8192 | tf_op jit(solution)/shard_map/all_to_all | solution.py:115
  34.7 1.5 copy-start.4
  37.3 10.4 %all-to-all-start = ((bf16[8,48,256]{2,1,0:T(8,128)(2,1)}), bf16[8,48,256]{2,1,0:T(8,128)(2,1)S(1)}, u32[]{:S(2)}, u32[]{:S(2)}) async-start(bf16[8,48,256]{2,1,0:T(8,128)(2,1)} %bitcast.19), calls=%async_computation | async-start | bytes 393216 | tf_op jit(solution)/shard_map/all_to_all | solution.py:114
  41.5 153.6 %all-reduce.33.cloned.1.call-start = ((), (), s32[]{:S(2)}) async-start(), calls=%async_computation.2 | async-start | bytes 2097152 | tf_op jit(solution)/shard_map/psum | solution.py:151
  47.9 147.3 %copy-start.2 = (f32[1024]{0:T(1024)S(1)}, f32[1024]{0:T(1024)}, u32[]{:S(2)}) copy-start(f32[1024]{0:T(1024)} %param.23) | copy-start | bytes 12292
  47.9 147.3 %copy-start.3 = (f32[1024]{0:T(1024)S(1)}, f32[1024]{0:T(1024)}, u32[]{:S(2)}) copy-start(f32[1024]{0:T(1024)} %param.22) | copy-start | bytes 12292
  137.9 1.0 copy-start.1
  139.0 93.3 %all-reduce.35.cloned.1.call-start = ((), (), s32[]{:S(2)}) async-start(), calls=%async_computation.3 | async-start | bytes 262144 | tf_op jit(solution)/shard_map/psum | solution.py:155
Sparse Core Ops, SparseCore 0:
  139.1 56.0 all-reduce.32
  198.3 33.8 all-reduce.34
where the time goes:
time: 244 us; the launch traced here: 241 us
  waiting for transfers between devices  96.3 us (39%)
  matrix products  56.6 us (23%)
  local copies, waits for them, and re-layouts  31.2 us (13%)
  starting transfers between devices  19.7 us (8%)
  between operations  14.6 us (6%)
  other arithmetic  14 us (6%)
  loops' own time  8.35 us (3%)
    psum x1, waiting for transfers between devices, per_device(): whole = lax.psum(total, 'terrain')  56.2 us
    dot_general x12, matrix products, add_block(): lax.dot_general(left, right, pick, preferred_element_type=jnp.float32)  55.5 us
    psum x1, waiting for transfers between devices, per_device(): portfolio = lax.psum(net_share, 'event') / (groups * lax.axis_size('event'))  34 us
    ge x12, local copies, waits for them, and re-layouts, add_block(): bin_range[None, None, :] >= threshold_part[:, :, None]  8.95 us
    broadcast_in_dim x12, local copies, waits for them, and re-layouts, add_block(): jnp.where(account_part[:, None] == columns[None, :], value_part[:, None],...  8.37 us
    another operation x1, loops' own time, per_device(): lax.scan(add_block, jnp.zeros((account_count, bin_count), jnp.float32), j...  8.35 us
    ppermute x2, starting transfers between devices, with_halo(): lax.ppermute(tail, axis, [(i, (i + 1) % count) for i in range(ends)])  7.51 us
    dynamic_slice x12, local copies, waits for them, and re-layouts, per_device(): lax.scan(add_block, jnp.zeros((account_count, bin_count), jnp.float32), j...  7.04 us
  transfers between devices with their start and end apart: 8, of which 3 were waited for; matrix products, arithmetic and copies ran while one was open for 6% of the time, Pallas kernels for 0%

commit v1 on v0

--- a/solution.py
+++ b/solution.py
@@ -152,7 +152,9 @@
     net_whole = jnp.minimum(jnp.maximum(whole * scale - deductible[:, None], 0.0), limit[:, None])
     net_loss = net_whole.astype(jnp.bfloat16)[None]
     net_share = lax.dynamic_slice_in_dim(net_whole, lower, share_rows, 0)
-    portfolio = lax.psum(net_share, "event") / (groups * lax.axis_size("event"))
+    portfolio = jnp.sum(lax.all_gather(net_share, "event"), axis=0) / (
+        groups * lax.axis_size("event")
+    )
     return (level, net_loss, portfolio)
 
 

time: 244 us -> 223 us (0.914)
  waiting for transfers between devices: 96.3 us -> 62.1 us
  blocking collectives: 0 us -> 14.9 us
    psum x1 -> x0, waiting for transfers between devices: 34 us -> none  [per_device(): portfolio = lax.psum(net_share, 'event') / (groups * lax.axis_size('event'))]
    all_gather x0 -> x1, blocking collectives: none -> 14.9 us  [per_device(): lax.all_gather(net_share, 'event')]
  transfers between devices with their start and end apart: 8 -> 7, of which waited for: 3 -> 2; matrix products, arithmetic and copies ran while one was open for 6% -> 6% of each run, Pallas kernels for 0% -> 0%
where the time goes in v1:
time: 223 us; the launch traced here: 220 us
  waiting for transfers between devices  62.1 us (28%)
  matrix products  56.6 us (25%)
  local copies, waits for them, and re-layouts  30.5 us (14%)
  starting transfers between devices  19.8 us (9%)
  blocking collectives  14.9 us (7%)
  between operations  14.6 us (7%)
  other arithmetic  13.1 us (6%)
  loops' own time  8.35 us (4%)
    psum x1, waiting for transfers between devices, per_device(): whole = lax.psum(total, 'terrain')  56.2 us
    dot_general x12, matrix products, add_block(): lax.dot_general(left, right, pick, preferred_element_type=jnp.float32)  55.5 us
    all_gather x1, blocking collectives, per_device(): lax.all_gather(net_share, 'event')  14.9 us
    ge x12, local copies, waits for them, and re-layouts, add_block(): bin_range[None, None, :] >= threshold_part[:, :, None]  8.95 us
    broadcast_in_dim x12, local copies, waits for them, and re-layouts, add_block(): jnp.where(account_part[:, None] == columns[None, :], value_part[:, None],...  8.37 us
    another operation x1, loops' own time, per_device(): lax.scan(add_block, jnp.zeros((account_count, bin_count), jnp.float32), j...  8.35 us
    ppermute x2, starting transfers between devices, with_halo(): lax.ppermute(tail, axis, [(i, (i + 1) % count) for i in range(ends)])  7.51 us
    dynamic_slice x12, local copies, waits for them, and re-layouts, per_device(): lax.scan(add_block, jnp.zeros((account_count, bin_count), jnp.float32), j...  7.04 us
  transfers between devices with their start and end apart: 7, of which 2 were waited for; matrix products, arithmetic and copies ran while one was open for 6% of the time, Pallas kernels for 0%

profile of v1, /device:TPU:0, one launch (start us, length us, event | category | flops | bytes accessed | tf_op | source)
XLA Modules:
  0.0 219.9 jit_solution(4470734225177594806)
XLA Ops:
  7.2 0.8 pad_maximum_fusion.3
  8.0 1.3 collective-permute-start.1
  9.3 3.0 %collective-permute-start = (f32[4,1,8,1024]{3,2,1,0:T(8,128)S(1)}, f32[4,1,8,1024]{3,2,1,0:T(8,128)S(1)}, u32[]{:S(2)}, u32[]{:S(2)}) collective-permute-start(f32[4,1,8,1024]{3,2,1,0:T(8,128)S(1)} %get-tuple-element.117), channel_id=1, source_target_pairs={{0,1},{1,2},{2,3},{3,4},{4,5},{5,6},{6,7},{8,9},{9,10},{10,11},{11... | collective-permute-start | bytes 393224 | tf_op jit(solution)/shard_map/ppermute | solution.py:19
  12.4 0.8 fusion.195
  13.2 4.5 %collective-permute-start.2 = (s32[1,8,1024]{2,1,0:T(8,128)S(1)}, s32[1,8,1024]{2,1,0:T(8,128)S(1)}, u32[]{:S(2)}, u32[]{:S(2)}) collective-permute-start(s32[1,8,1024]{2,1,0:T(8,128)S(1)} %get-tuple-element.152), channel_id=1, source_target_pairs={{0,1},{1,2},{2,3},{3,4},{4,5},{5,6},{6,7},{8,9},{9,10},{10,11},{11... | collective-permute-start | bytes 98312 | tf_op jit(solution)/shard_map/ppermute | solution.py:19
  17.7 1.3 collective-permute-start.3
  20.5 0.8 fusion.174
  22.7 5.3 %all-to-all-start.1 = ((bf16[8,1,48]{2,1,0:T(2,128)(2,1)}), bf16[8,1,48]{2,1,0:T(2,128)(2,1)S(1)}, u32[]{:S(2)}, u32[]{:S(2)}) async-start(bf16[8,1,48]{2,1,0:T(2,128)(2,1)} %convert_element_type.186), calls=%async_computation.1 | async-start | bytes 8192 | tf_op jit(solution)/shard_map/all_to_all | solution.py:115
  28.2 0.9 constant_dynamic-update-slice_fusion.1
  29.2 1.0 pad_maximum_fusion
  35.3 0.9 fusion.184
  36.2 1.1 convolution_convert_fusion
  37.3 4.2 %all-to-all-start = ((bf16[8,48,256]{2,1,0:T(8,128)(2,1)}), bf16[8,48,256]{2,1,0:T(8,128)(2,1)S(1)}, u32[]{:S(2)}, u32[]{:S(2)}) async-start(bf16[8,48,256]{2,1,0:T(8,128)(2,1)} %bitcast.19), calls=%async_computation | async-start | bytes 393216 | tf_op jit(solution)/shard_map/all_to_all | solution.py:114
  41.9 5.9 %all-to-all-done = bf16[8,48,256]{2,1,0:T(8,128)(2,1)S(1)} async-done(((bf16[8,48,256]{2,1,0:T(8,128)(2,1)}), bf16[8,48,256]{2,1,0:T(8,128)(2,1)S(1)}, u32[]{:S(2)}, u32[]{:S(2)}) %all-to-all-start) | async-done | bytes 196640 | tf_op jit(solution)/shard_map/all_to_all | solution.py:114
  47.9 90.0 %while.11 = (s32[]{:T(128)}, f32[1024,256]{1,0:T(8,128)S(1)}, s32[12]{0:T(128)S(1)}, s32[384,128]{1,0:T(8,128)}, bf16[384,128]{1,0:T(8,128)(2,1)}, /*index=5*/s3...) while((s32[]{:T(128)}, f32[1024,256]{1,0:T(8,128)S(1)}, ...), condition=%wide.region_5.6_spmd.clone, body=%wide.region_4.5_spmd.clone.sunk | while | flops 2158493696 | bytes 6463685 | solution.py:146
  50.8 4.6 %fusion.203 = f32[1024,256]{1,0:T(8,128)S(1)} fusion(bf16[4096,256]{1,0:T(8,128)(2,1)S(1)} %bitcast.78, s32[4096]{0:T(1024)S(1)} %get-tuple-element.201, s32[4096]{0:T(1024)S(1)} %get-tuple-element.202, bf16[4096]{0:T(1024)(128)(2,1)S(1)} %dynamic-slice_bitcast_fusion.6, f32[1024,256]{1,0:T(8,128)S(1)} %get-tuple-element.215, pred[]{:T(512)S(6)} %compare.53), kind=kOutput, calls=%fused_computation.11.clone.1 | convolution fusion | flops 2158493696 | bytes 4235265 | tf_op jit(solution)/shard_map/while/body/eval_jaxpr/dot_general | solution.py:142
  58.3 4.6 %fusion.203 = f32[1024,256]{1,0:T(8,128)S(1)} fusion(bf16[4096,256]{1,0:T(8,128)(2,1)S(1)} %bitcast.78, s32[4096]{0:T(1024)S(1)} %get-tuple-element.201, s32[4096]{0:T(1024)S(1)} %get-tuple-element.202, bf16[4096]{0:T(1024)(128)(2,1)S(1)} %dynamic-slice_bitcast_fusion.6, f32[1024,256]{1,0:T(8,128)S(1)} %get-tuple-element.215, pred[]{:T(512)S(6)} %compare.53), kind=kOutput, calls=%fused_computation.11.clone.1 | convolution fusion | flops 2158493696 | bytes 4235265 | tf_op jit(solution)/shard_map/while/body/eval_jaxpr/dot_general | solution.py:142
  64.3 0.7 dynamic-slice_bitcast_fusion.5
  65.8 4.6 %fusion.203 = f32[1024,256]{1,0:T(8,128)S(1)} fusion(bf16[4096,256]{1,0:T(8,128)(2,1)S(1)} %bitcast.78, s32[4096]{0:T(1024)S(1)} %get-tuple-element.201, s32[4096]{0:T(1024)S(1)} %get-tuple-element.202, bf16[4096]{0:T(1024)(128)(2,1)S(1)} %dynamic-slice_bitcast_fusion.6, f32[1024,256]{1,0:T(8,128)S(1)} %get-tuple-element.215, pred[]{:T(512)S(6)} %compare.53), kind=kOutput, calls=%fused_computation.11.clone.1 | convolution fusion | flops 2158493696 | bytes 4235265 | tf_op jit(solution)/shard_map/while/body/eval_jaxpr/dot_general | solution.py:142
  73.3 4.6 %fusion.203 = f32[1024,256]{1,0:T(8,128)S(1)} fusion(bf16[4096,256]{1,0:T(8,128)(2,1)S(1)} %bitcast.78, s32[4096]{0:T(1024)S(1)} %get-tuple-element.201, s32[4096]{0:T(1024)S(1)} %get-tuple-element.202, bf16[4096]{0:T(1024)(128)(2,1)S(1)} %dynamic-slice_bitcast_fusion.6, f32[1024,256]{1,0:T(8,128)S(1)} %get-tuple-element.215, pred[]{:T(512)S(6)} %compare.53), kind=kOutput, calls=%fused_computation.11.clone.1 | convolution fusion | flops 2158493696 | bytes 4235265 | tf_op jit(solution)/shard_map/while/body/eval_jaxpr/dot_general | solution.py:142
  80.8 4.6 %fusion.203 = f32[1024,256]{1,0:T(8,128)S(1)} fusion(bf16[4096,256]{1,0:T(8,128)(2,1)S(1)} %bitcast.78, s32[4096]{0:T(1024)S(1)} %get-tuple-element.201, s32[4096]{0:T(1024)S(1)} %get-tuple-element.202, bf16[4096]{0:T(1024)(128)(2,1)S(1)} %dynamic-slice_bitcast_fusion.6, f32[1024,256]{1,0:T(8,128)S(1)} %get-tuple-element.215, pred[]{:T(512)S(6)} %compare.53), kind=kOutput, calls=%fused_computation.11.clone.1 | convolution fusion | flops 2158493696 | bytes 4235265 | tf_op jit(solution)/shard_map/while/body/eval_jaxpr/dot_general | solution.py:142
  88.3 4.6 %fusion.203 = f32[1024,256]{1,0:T(8,128)S(1)} fusion(bf16[4096,256]{1,0:T(8,128)(2,1)S(1)} %bitcast.78, s32[4096]{0:T(1024)S(1)} %get-tuple-element.201, s32[4096]{0:T(1024)S(1)} %get-tuple-element.202, bf16[4096]{0:T(1024)(128)(2,1)S(1)} %dynamic-slice_bitcast_fusion.6, f32[1024,256]{1,0:T(8,128)S(1)} %get-tuple-element.215, pred[]{:T(512)S(6)} %compare.53), kind=kOutput, calls=%fused_computation.11.clone.1 | convolution fusion | flops 2158493696 | bytes 4235265 | tf_op jit(solution)/shard_map/while/body/eval_jaxpr/dot_general | solution.py:142
  95.8 4.6 %fusion.203 = f32[1024,256]{1,0:T(8,128)S(1)} fusion(bf16[4096,256]{1,0:T(8,128)(2,1)S(1)} %bitcast.78, s32[4096]{0:T(1024)S(1)} %get-tuple-element.201, s32[4096]{0:T(1024)S(1)} %get-tuple-element.202, bf16[4096]{0:T(1024)(128)(2,1)S(1)} %dynamic-slice_bitcast_fusion.6, f32[1024,256]{1,0:T(8,128)S(1)} %get-tuple-element.215, pred[]{:T(512)S(6)} %compare.53), kind=kOutput, calls=%fused_computation.11.clone.1 | convolution fusion | flops 2158493696 | bytes 4235265 | tf_op jit(solution)/shard_map/while/body/eval_jaxpr/dot_general | solution.py:142
  103.3 4.6 %fusion.203 = f32[1024,256]{1,0:T(8,128)S(1)} fusion(bf16[4096,256]{1,0:T(8,128)(2,1)S(1)} %bitcast.78, s32[4096]{0:T(1024)S(1)} %get-tuple-element.201, s32[4096]{0:T(1024)S(1)} %get-tuple-element.202, bf16[4096]{0:T(1024)(128)(2,1)S(1)} %dynamic-slice_bitcast_fusion.6, f32[1024,256]{1,0:T(8,128)S(1)} %get-tuple-element.215, pred[]{:T(512)S(6)} %compare.53), kind=kOutput, calls=%fused_computation.11.clone.1 | convolution fusion | flops 2158493696 | bytes 4235265 | tf_op jit(solution)/shard_map/while/body/eval_jaxpr/dot_general | solution.py:142
  110.8 4.6 %fusion.203 = f32[1024,256]{1,0:T(8,128)S(1)} fusion(bf16[4096,256]{1,0:T(8,128)(2,1)S(1)} %bitcast.78, s32[4096]{0:T(1024)S(1)} %get-tuple-element.201, s32[4096]{0:T(1024)S(1)} %get-tuple-element.202, bf16[4096]{0:T(1024)(128)(2,1)S(1)} %dynamic-slice_bitcast_fusion.6, f32[1024,256]{1,0:T(8,128)S(1)} %get-tuple-element.215, pred[]{:T(512)S(6)} %compare.53), kind=kOutput, calls=%fused_computation.11.clone.1 | convolution fusion | flops 2158493696 | bytes 4235265 | tf_op jit(solution)/shard_map/while/body/eval_jaxpr/dot_general | solution.py:142
  118.3 4.6 %fusion.203 = f32[1024,256]{1,0:T(8,128)S(1)} fusion(bf16[4096,256]{1,0:T(8,128)(2,1)S(1)} %bitcast.78, s32[4096]{0:T(1024)S(1)} %get-tuple-element.201, s32[4096]{0:T(1024)S(1)} %get-tuple-element.202, bf16[4096]{0:T(1024)(128)(2,1)S(1)} %dynamic-slice_bitcast_fusion.6, f32[1024,256]{1,0:T(8,128)S(1)} %get-tuple-element.215, pred[]{:T(512)S(6)} %compare.53), kind=kOutput, calls=%fused_computation.11.clone.1 | convolution fusion | flops 2158493696 | bytes 4235265 | tf_op jit(solution)/shard_map/while/body/eval_jaxpr/dot_general | solution.py:142
  125.8 4.6 %fusion.203 = f32[1024,256]{1,0:T(8,128)S(1)} fusion(bf16[4096,256]{1,0:T(8,128)(2,1)S(1)} %bitcast.78, s32[4096]{0:T(1024)S(1)} %get-tuple-element.201, s32[4096]{0:T(1024)S(1)} %get-tuple-element.202, bf16[4096]{0:T(1024)(128)(2,1)S(1)} %dynamic-slice_bitcast_fusion.6, f32[1024,256]{1,0:T(8,128)S(1)} %get-tuple-element.215, pred[]{:T(512)S(6)} %compare.53), kind=kOutput, calls=%fused_computation.11.clone.1 | convolution fusion | flops 2158493696 | bytes 4235265 | tf_op jit(solution)/shard_map/while/body/eval_jaxpr/dot_general | solution.py:142
  133.3 4.6 %fusion.203 = f32[1024,256]{1,0:T(8,128)S(1)} fusion(bf16[4096,256]{1,0:T(8,128)(2,1)S(1)} %bitcast.78, s32[4096]{0:T(1024)S(1)} %get-tuple-element.201, s32[4096]{0:T(1024)S(1)} %get-tuple-element.202, bf16[4096]{0:T(1024)(128)(2,1)S(1)} %dynamic-slice_bitcast_fusion.6, f32[1024,256]{1,0:T(8,128)S(1)} %get-tuple-element.215, pred[]{:T(512)S(6)} %compare.53), kind=kOutput, calls=%fused_computation.11.clone.1 | convolution fusion | flops 2158493696 | bytes 4235265 | tf_op jit(solution)/shard_map/while/body/eval_jaxpr/dot_general | solution.py:142
  137.9 1.0 copy-done.1
  138.9 56.2 %all-reduce.32.cloned.1.call-done = f32[1024,256]{1,0:T(8,128)} async-done(((f32[1024,256]{1,0:T(8,128)}), f32[1024,256]{1,0:T(8,128)}) %all-reduce.32.cloned.1.call-update) | async-done | bytes 1048592 | tf_op jit(solution)/shard_map/psum | solution.py:151
  195.2 2.4 %convert_bitcast_fusion = (bf16[1,1024,256]{2,1,0:T(8,128)(2,1)}, f32[1024,256]{1,0:T(8,128)S(1)}) fusion(f32[1024]{0:T(1024)S(1)} %copy-done.2, f32[1024]{0:T(1024)S(1)} %copy-done.3, f32[1024,256]{1,0:T(8,128)} %all-reduce.32.cloned.1.call-done), kind=kLoop, calls=%fused_computation.29 | loop fusion | flops 1310720 | bytes 2629632 | tf_op jit(solution)/shard_map/broadcast_in_dim | solution.py:153
  197.5 14.9 %all-gather = f32[512,256]{1,0:T(8,128)S(1)} all-gather(f32[128,256]{1,0:T(8,128)S(1)} %constant_dynamic-slice_fusion.1), channel_id=2, replica_groups=mesh['event'=4,'terrain'=8] {'event'}, dimensions={0}, use_global_device_ids=true | all-gather | bytes 655360 | tf_op jit(solution)/shard_map/all_gather | solution.py:155
  (143 shorter events, 34.6 us)
Async XLA Ops:
  7.2 29.1 %copy-start = (bf16[128,256]{1,0:T(8,128)(2,1)S(1)}, bf16[128,256]{1,0:T(8,128)(2,1)}, u32[]{:S(2)}) copy-start(bf16[128,256]{1,0:T(8,128)(2,1)} %param.17) | copy-start | bytes 196612
  8.0 21.1 %collective-permute-start.1 = (f32[4,1,8,1024]{3,2,1,0:T(8,128)S(1)}, f32[4,1,8,1024]{3,2,1,0:T(8,128)S(1)}, u32[]{:S(2)}, u32[]{:S(2)}) collective-permute-start(f32[4,1,8,1024]{3,2,1,0:T(8,128)S(1)} %get-tuple-element.118), channel_id=1, source_target_pairs={{1,0},{2,1},{3,2},{4,3},{5,4},{6,5},{7,6},{9,8},{10,9},{11,10},{12... | collective-permute-start | bytes 393224 | tf_op jit(solution)/shard_map/ppermute | solution.py:21
  9.3 19.8 %collective-permute-start = (f32[4,1,8,1024]{3,2,1,0:T(8,128)S(1)}, f32[4,1,8,1024]{3,2,1,0:T(8,128)S(1)}, u32[]{:S(2)}, u32[]{:S(2)}) collective-permute-start(f32[4,1,8,1024]{3,2,1,0:T(8,128)S(1)} %get-tuple-element.117), channel_id=1, source_target_pairs={{0,1},{1,2},{2,3},{3,4},{4,5},{5,6},{6,7},{8,9},{9,10},{10,11},{11... | collective-permute-start | bytes 393224 | tf_op jit(solution)/shard_map/ppermute | solution.py:19
  13.2 15.0 %collective-permute-start.2 = (s32[1,8,1024]{2,1,0:T(8,128)S(1)}, s32[1,8,1024]{2,1,0:T(8,128)S(1)}, u32[]{:S(2)}, u32[]{:S(2)}) collective-permute-start(s32[1,8,1024]{2,1,0:T(8,128)S(1)} %get-tuple-element.152), channel_id=1, source_target_pairs={{0,1},{1,2},{2,3},{3,4},{4,5},{5,6},{6,7},{8,9},{9,10},{10,11},{11... | collective-permute-start | bytes 98312 | tf_op jit(solution)/shard_map/ppermute | solution.py:19
  17.7 11.5 %collective-permute-start.3 = (s32[1,8,1024]{2,1,0:T(8,128)S(1)}, s32[1,8,1024]{2,1,0:T(8,128)S(1)}, u32[]{:S(2)}, u32[]{:S(2)}) collective-permute-start(s32[1,8,1024]{2,1,0:T(8,128)S(1)} %get-tuple-element.151), channel_id=1, source_target_pairs={{1,0},{2,1},{3,2},{4,3},{5,4},{6,5},{7,6},{9,8},{10,9},{11,10},{12... | collective-permute-start | bytes 98312 | tf_op jit(solution)/shard_map/ppermute | solution.py:21
  22.7 14.6 %all-to-all-start.1 = ((bf16[8,1,48]{2,1,0:T(2,128)(2,1)}), bf16[8,1,48]{2,1,0:T(2,128)(2,1)S(1)}, u32[]{:S(2)}, u32[]{:S(2)}) async-start(bf16[8,1,48]{2,1,0:T(2,128)(2,1)} %convert_element_type.186), calls=%async_computation.1 | async-start | bytes 8192 | tf_op jit(solution)/shard_map/all_to_all | solution.py:115
  34.7 1.5 copy-start.4
  37.3 10.4 %all-to-all-start = ((bf16[8,48,256]{2,1,0:T(8,128)(2,1)}), bf16[8,48,256]{2,1,0:T(8,128)(2,1)S(1)}, u32[]{:S(2)}, u32[]{:S(2)}) async-start(bf16[8,48,256]{2,1,0:T(8,128)(2,1)} %bitcast.19), calls=%async_computation | async-start | bytes 393216 | tf_op jit(solution)/shard_map/all_to_all | solution.py:114
  41.5 153.6 %all-reduce.32.cloned.1.call-start = ((), (), s32[]{:S(2)}) async-start(), calls=%async_computation.2 | async-start | bytes 2097152 | tf_op jit(solution)/shard_map/psum | solution.py:151
  47.9 147.3 %copy-start.2 = (f32[1024]{0:T(1024)S(1)}, f32[1024]{0:T(1024)}, u32[]{:S(2)}) copy-start(f32[1024]{0:T(1024)} %param.23) | copy-start | bytes 12292
  47.9 147.3 %copy-start.3 = (f32[1024]{0:T(1024)S(1)}, f32[1024]{0:T(1024)}, u32[]{:S(2)}) copy-start(f32[1024]{0:T(1024)} %param.22) | copy-start | bytes 12292
  137.9 1.0 copy-start.1
Sparse Core Ops, SparseCore 0:
  139.1 56.0 all-reduce.31
